TPU v7x, 32 devices: a whole 2x2x4 slice. The times are simulated.
32 devices in a mesh: groups: 2 (over y), cells: 4 (over z), obs: 2 (over x), mem: 2 (over core).
Axes of the slice: x: 2, y: 2, z: 4, core: 2. Of those that a mesh axis runs over, the one named last changes fastest.
Arguments:
- members: bfloat16 [64, 32768], P('mem', ('groups', 'cells', 'obs')), parts along dimension 1, may hold values from -4 to 4
- observed: float32 [16384], P(('groups', 'cells', 'obs')), parts along dimension 0, may hold values from -6 to 6
- obs_error: float32 [16384], P(('groups', 'cells', 'obs')), parts along dimension 0, may hold values from 0.25 to 2
- obs_cells: int32 [16384], P(('groups', 'cells', 'obs')), parts along dimension 0, may hold values from 0 to 2047
- perturbations: bfloat16 [16384, 64], P(('groups', 'cells', 'obs')), parts along dimension 0, may hold values from -5 to 5
- region_ids: int32 [64], P(('groups', 'cells', 'obs')), parts along dimension 0, may hold values from 0 to 3
Outputs:
- updated: bfloat16 [64, 32768], P('mem', ('groups', 'cells', 'obs')), parts along dimension 1
There are 2 independent parts, one for each index of `groups`. A program takes and returns all parts, laid end to end along the dimension named above; each array names one. Nothing has to cross between parts.
Inputs may be any that keep to these rules, and one draw needn't show every extreme that they name: obs_cells[j] names a cell of section j // 1024, the cells s * 2048 to (s + 1) * 2048 - 1 forming section s. `region_ids`: block b holds the cells b * 512 to (b + 1) * 512 - 1.
All inputs are finite; a program needn't handle non-finite values.
Results may differ from a plain program's by a relative error of at most 0.006.
Values may be sent and summed in bfloat16 or wider, within the bound.
A program may use at most 64 MiB of HBM per device.

v0:
```python
import jax
import jax.numpy as jnp
from jax import lax
from jax.sharding import PartitionSpec as P

NE = 64
BLOCK = 512
NLOC = 4


def solve_regions(sens_gram, cross, misfit):
    damping = NE - 1.0 + misfit / NE
    eye = jnp.eye(NE, dtype=jnp.float32)
    system = sens_gram + damping[:, None, None] * eye[None, :, :]
    factor = jnp.linalg.cholesky(system)
    return jax.vmap(lambda fac, rhs: jax.scipy.linalg.cho_solve((fac, True), rhs))(factor, cross)


def body(members, observed, obs_error, obs_cells, perturbations, region_ids):
    half_members = members.shape[0]
    cell_rows = members.shape[1]
    blocks = region_ids.shape[0]
    mem_index = lax.axis_index("mem")
    part_rows = observed.shape[0] // lax.axis_size("mem")
    row_start = mem_index * part_rows
    my_cells = lax.dynamic_slice_in_dim(obs_cells, row_start, part_rows)
    my_obs = lax.dynamic_slice_in_dim(observed, row_start, part_rows)
    my_error = lax.dynamic_slice_in_dim(obs_error, row_start, part_rows)
    my_noise = lax.dynamic_slice_in_dim(perturbations, row_start, part_rows, 0)
    block_onehot = (region_ids[:, None] == jnp.arange(NLOC, dtype=jnp.int32)[None, :]).astype(
        jnp.float32
    )
    obs_block = (my_cells // BLOCK)[:, None] == jnp.arange(blocks, dtype=jnp.int32)[None, :]
    obs_onehot = jnp.dot(
        obs_block.astype(jnp.float32), block_onehot, precision=lax.Precision.HIGHEST
    )
    obs_mask = obs_onehot.astype(jnp.bfloat16)
    ensemble = members
    whole = lax.all_gather(ensemble, "mem", axis=0, tiled=True)
    center = jnp.sum(whole.astype(jnp.float32), axis=0) / NE
    anomaly = (whole.astype(jnp.float32) - center[None, :]).astype(jnp.bfloat16)
    values = jnp.take(whole, my_cells, axis=1).T.astype(jnp.float32)
    predicted = values + 0.2 * values * values * values
    pmean = jnp.sum(predicted, axis=1) / NE
    sens = ((predicted - pmean[:, None]) / my_error[:, None]).astype(jnp.bfloat16)
    innov = (my_obs[:, None] - predicted) / my_error[:, None] + my_noise.astype(jnp.float32)
    innov_b = innov.astype(jnp.bfloat16)
    masked = (sens[:, None, :] * obs_mask[:, :, None]).reshape(part_rows, NLOC * NE)
    joined = jnp.concatenate([sens, innov_b], axis=1)
    gram = lax.dot_general(
        masked, joined, (((0,), (0,)), ((), ())), preferred_element_type=jnp.float32
    )
    gram = gram.reshape(NLOC, NE, 2 * NE)
    misfit = jnp.dot(jnp.sum(innov * innov, axis=1), obs_onehot, precision=lax.Precision.HIGHEST)
    gram, misfit = (
        lax.psum_scatter(gram, "obs", scatter_dimension=0, tiled=True),
        lax.psum_scatter(misfit, "obs", scatter_dimension=0, tiled=True),
    )
    gram, misfit = lax.psum((gram, misfit), ("cells", "mem"))
    coeff = solve_regions(gram[:, :, :NE], gram[:, :, NE:], misfit)
    mine = lax.dynamic_slice_in_dim(coeff, mem_index * half_members, half_members, 2).astype(
        jnp.bfloat16
    )
    mine = lax.all_gather(mine, "obs", axis=0, tiled=True)
    chosen = jnp.einsum(
        "bn,nef->bef", block_onehot, mine.astype(jnp.float32), precision=lax.Precision.HIGHEST
    ).astype(jnp.bfloat16)
    delta = jnp.einsum(
        "ebc,bef->fbc",
        anomaly.reshape(NE, blocks, BLOCK),
        chosen,
        preferred_element_type=jnp.float32,
    )
    ensemble = (ensemble.astype(jnp.float32) + delta.reshape(half_members, cell_rows)).astype(
        jnp.bfloat16
    )
    return ensemble


def solution(mesh):
    in_specs = (
        P("mem", ("groups", "cells", "obs")),
        P(("groups", "cells", "obs")),
        P(("groups", "cells", "obs")),
        P(("groups", "cells", "obs")),
        P(("groups", "cells", "obs"), None),
        P(("groups", "cells", "obs")),
    )
    out_specs = P("mem", ("groups", "cells", "obs"))
    return jax.shard_map(body, mesh=mesh, in_specs=in_specs, out_specs=out_specs, check_vma=False)
```

profile of v0, /device:TPU:0, one launch (start us, length us, event | category | flops | bytes accessed | tf_op | source)
XLA Modules:
  0.0 129.3 jit_solution(6274415740971316114)
XLA Ops:
  6.5 0.0 reduce-scatter.2.cloned.1.call-start
  6.5 0.0 copy-start.3
  6.5 0.7 copy-done.3
  7.2 0.1 compare_and_fusion
  7.3 0.1 add_select_fusion
  7.4 2.3 %all_gather.6 = bf16[64,2048]{1,0:T(8,128)(2,1)S(1)} all-gather(bf16[32,2048]{1,0:T(8,128)(2,1)} %param.6), channel_id=1, replica_groups=mesh['groups'=2,'cells'=4,'obs'=2,'mem'=2] {'mem'}, dimensions={0}, use_global_device_ids=true | all-gather | bytes 393216 | tf_op jit(solution)/shard_map/all_gather | solution.py:39
  9.7 0.3 copy.50
  10.0 1.3 %gather_fusion = bf16[512,64]{1,0:T(8,128)(2,1)S(1)} fusion(bf16[64,2048]{0,1:T(8,128)(2,1)S(1)} %copy.50, s32[1024]{0:T(1024)S(1)} %pad_clamp_fusion), kind=kCustom, calls=%fused_computation | custom fusion | bytes 133120 | tf_op jit(solution)/shard_map/jit(_take)/gather | solution.py:42
  11.4 0.0 copy-start.4
  11.4 0.0 copy-start.2
  11.4 0.1 copy.51
  11.5 0.6 copy-done.4
  12.0 0.0 copy-start.5
  12.0 0.1 dynamic_slice.16
  12.1 0.6 copy-done.5
  12.7 0.1 dynamic_slice.17
  12.8 0.0 copy-done.2
  12.8 0.1 multiply_reduce_fusion
  12.9 0.0 copy-start.6
  13.0 0.6 copy-done.6
  13.6 0.3 fusion.36
  13.8 1.0 fusion.3
  14.8 0.0 reduce-scatter.2.cloned.1.call-update
  14.8 0.0 all-reduce.3.cloned.1.call-start
  14.9 0.1 convert_reduce_fusion
  14.9 0.1 convolution_bitcast_fusion.1
  15.1 5.7 %all-reduce = f32[4]{0:T(128)S(1)} all-reduce(f32[4]{0:T(128)S(1)} %convolution_bitcast_fusion.1), channel_id=3, replica_groups=mesh['groups'=2,'cells'=4,'obs'=2,'mem'=2] {'obs'}, use_global_device_ids=true, to_apply=%region_4.5.clone | all-reduce | flops 4 | bytes 32
  20.8 0.1 fusion
  20.9 0.0 copy-start.7
  20.9 0.6 copy-done.7
  21.5 0.6 dynamic-slice
  22.8 0.1 dynamic-slice.1
  22.9 16.3 %psum.15 = f32[2]{0:T(128)S(1)} all-reduce(f32[2]{0:T(128)S(1)} %dynamic-slice.1), channel_id=1, replica_groups=mesh['groups'=2,'cells'=4,'obs'=2,'mem'=2] {'cells','mem'}, use_global_device_ids=true, to_apply=%region_5.6 | all-reduce | flops 2 | bytes 16 | tf_op jit(solution)/shard_map/psum | solution.py:59
  39.2 0.0 reduce-scatter.2.cloned.1.call-done
  39.2 0.0 all-reduce.3.cloned.1.call-update
  39.3 0.1 copy.54
  39.3 53.3 %all-reduce.3.cloned.1.call-done = f32[2,64,128]{1,2,0:T(8,128)} async-done(((f32[2,64,128]{1,2,0:T(8,128)}), f32[2,64,128]{1,2,0:T(8,128)}) %all-reduce.3.cloned.1.call-update) | async-done | bytes 65552 | tf_op jit(solution)/shard_map/psum | solution.py:59
  92.6 0.0 copy-start.1
  92.6 1.0 slice_add_fusion
  93.6 0.1 copy.55
  93.7 0.0 copy-done.1
  93.7 0.1 fusion.24
  93.8 11.7 %custom-call.11 = f32[2,64,64]{2,1,0:T(8,128)S(1)} custom-call(f32[2,64,64]{2,1,0:T(8,128)S(1)} %fusion.24), custom_call_target="Cholesky" | custom-call | tf_op jit(solution)/shard_map/jit(cholesky)/cholesky | solution.py:15
  105.5 0.1 compare_reduce_fusion
  105.7 0.1 select_bitcast_fusion
  105.7 9.8 %custom-call.12 = f32[2,1,64,64]{2,3,1,0:T(8,128)S(1)} custom-call(f32[2,1,64,64]{3,2,1,0:T(8,128)S(1)} %select_bitcast_fusion), custom_call_target="InvertDiagBlocksLowerTriangular" | custom-call | tf_op jit(solution)/shard_map/vmap(jit(_cho_solve))/triangular_solve | solution.py:16
  115.6 0.2 fusion.19
  115.8 0.2 fusion.21
  116.1 4.4 %all_gather.7 = bf16[4,64,32]{1,2,0:T(8,128)(2,1)S(1)} all-gather(bf16[2,64,32]{1,2,0:T(8,128)(2,1)S(1)} %dynamic-slice_convert_fusion), channel_id=1, replica_groups=mesh['groups'=2,'cells'=4,'obs'=2,'mem'=2] {'obs'}, dimensions={0}, use_global_device_ids=true | all-gather | bytes 24576 | tf_op jit(solution)/shard_map/all_gather | solution.py:64
  120.5 0.2 convolution_convert_fusion
  120.7 0.2 convolution_bitcast_fusion
  120.8 0.0 copy-start
  120.9 0.9 copy-done
  121.8 0.7 add_convert_fusion
  (11 shorter events, 0.2 us)
Async XLA Ops:
  6.5 32.7 %reduce-scatter.2.cloned.1.call-start = ((), (), s32[]{:S(2)}) async-start(), calls=%async_computation.1 | async-start | bytes 393216 | tf_op jit(solution)/shard_map/reduce_scatter | solution.py:56
  6.5 0.7 copy-start.3
  11.4 0.7 copy-start.4
  11.4 1.4 %copy-start.2 = (bf16[1024,64]{0,1:T(8,128)(2,1)S(1)}, bf16[1024,64]{0,1:T(8,128)(2,1)}, u32[]{:S(2)}) copy-start(bf16[1024,64]{0,1:T(8,128)(2,1)} %param.10) | copy-start | bytes 393220
  12.0 0.7 copy-start.5
  12.9 0.7 copy-start.6
  14.8 77.8 %all-reduce.3.cloned.1.call-start = ((), (), s32[]{:S(2)}) async-start(), calls=%async_computation.2 | async-start | bytes 262144 | tf_op jit(solution)/shard_map/psum | solution.py:59
  20.9 0.7 copy-start.7
  92.6 1.1 copy-start.1
  120.8 0.9 copy-start
Sparse Core Ops, SparseCore 0:
  14.9 14.3 reduce-scatter.1
  39.4 53.1 all-reduce.2
where the time goes:
time: 130 us; the launch traced here: 129 us
  waiting for transfers between devices  53.3 us (41%)
  blocking collectives  28.8 us (22%)
  other arithmetic  24 us (18%)
  between operations  14.3 us (11%)
  local copies, waits for them, and re-layouts  6.69 us (5%)
  matrix products  2.2 us (2%)
    psum x1, waiting for transfers between devices, body(): gram, misfit = lax.psum((gram, misfit), ('cells', 'mem'))  53.3 us
    psum x1, blocking collectives, body(): gram, misfit = lax.psum((gram, misfit), ('cells', 'mem'))  16.3 us
    another operation x4, other arithmetic, solve_regions(): factor = jnp.linalg.cholesky(system)  11.9 us
    another operation x3, other arithmetic, solve_regions(): jax.scipy.linalg.cho_solve((fac, True), rhs)  9.92 us
    unnamed x1, blocking collectives  5.74 us
    unnamed x18, local copies, waits for them, and re-layouts  4.65 us
    all_gather x1, blocking collectives, body(): mine = lax.all_gather(mine, 'obs', axis=0, tiled=True)  4.41 us
  transfers between devices with their start and end apart: 2, of which 1 were waited for; matrix products, arithmetic and copies ran while one was open for 1% of the time, Pallas kernels for 0%

commit v1 on v0

v1 whole, which is shorter than its diff:
```python
import functools

import jax
import jax.numpy as jnp
from jax import lax
from jax.experimental import pallas as pl
from jax.experimental.pallas import tpu as pltpu
from jax.sharding import PartitionSpec as P

BLOCK = 512
NLOC = 4
LANE = 128
MESH = pl.DeviceIdType.MESH


def gather_lanes(table, cells):
    rows, width = table.shape
    columns = []
    for start in range(0, cells.shape[1], LANE):
        index = cells[:, start : start + LANE]
        low = jnp.broadcast_to(index % LANE, (rows, LANE))
        high = jnp.broadcast_to(index // LANE, (rows, LANE))
        total = None
        for part in range(width // LANE):
            found = jnp.take_along_axis(
                table[:, part * LANE : (part + 1) * LANE], low, axis=1, mode="promise_in_bounds"
            )
            total = found if total is None else jnp.where(high == part, found, total)
        columns.append(total)
    return jnp.concatenate(columns, axis=1)


def eliminate(rows, ne):
    groups = len(rows)
    sub = lax.broadcasted_iota(jnp.int32, rows[0].shape, 0)
    for block in range(groups):
        base = block * 8
        cols = [
            [jnp.broadcast_to(rows[g][:, base + j : base + j + 1], rows[g].shape) for g in range(groups)]
            for j in range(8)
        ]
        for j in range(8):
            inv = 1.0 / cols[j][block][j : j + 1, :]
            here = sub == j
            for l in range(j + 1, 8):
                factor = cols[l][block][j : j + 1, :] * inv
                for g in range(groups):
                    new = cols[l][g] - cols[j][g] * factor
                    cols[l][g] = jnp.where(here, factor, new) if g == block else new
            pivot_row = rows[block][j : j + 1, :] * inv
            for g in range(groups):
                new = rows[g] - cols[j][g] * pivot_row
                rows[g] = jnp.where(here, pivot_row, new) if g == block else new
    return rows


def kernel(
    nz, nx, nm, region_ref, members_ref, observed_ref, error_ref, cells_ref, noise_ref, out_ref,
    vals, whole, mine, slots, coeff,
    v_send, v_recv, w_send, w_recv, g_send, g_recv, c_send, c_recv,
):
    z, x, m = lax.axis_index("cells"), lax.axis_index("obs"), lax.axis_index("mem")
    half = members_ref.shape[0]
    ne = half * nm
    nreg = NLOC // nm
    chips = nz * nx
    blocks = region_ref.shape[0]

    def chip(offset):
        return {"cells": lax.rem(z + offset // nx, nz), "obs": lax.rem(x + offset % nx, nx)}

    def core(offset):
        return {"mem": lax.rem(m + offset, nm)}

    barrier = pltpu.get_barrier_semaphore()
    for offset in range(1, nm):
        pl.semaphore_signal(barrier, inc=1, device_id=core(offset), device_id_type=MESH)
    for offset in range(1, chips):
        pl.semaphore_signal(barrier, inc=1, device_id=chip(offset), device_id_type=MESH)

    own = pl.ds(pl.multiple_of(m * half, half), half)
    cells = cells_ref[...]
    members = members_ref[...]
    vals[own, :] = gather_lanes(members.astype(jnp.float32), cells).astype(jnp.bfloat16)

    pl.semaphore_wait(barrier, nm - 1 + chips - 1)
    swaps = []
    for offset in range(1, nm):
        swaps.append(
            pltpu.make_async_remote_copy(
                src_ref=vals.at[own], dst_ref=vals.at[own],
                send_sem=v_send.at[offset - 1], recv_sem=v_recv.at[offset - 1],
                device_id=core(offset), device_id_type=MESH,
            )
        )
        swaps[-1].start()
    fetches = []
    for offset in range(1, nm):
        fetches.append(
            pltpu.make_async_remote_copy(
                src_ref=members_ref, dst_ref=whole.at[own],
                send_sem=w_send.at[offset - 1], recv_sem=w_recv.at[offset - 1],
                device_id=core(offset), device_id_type=MESH,
            )
        )
        fetches[-1].start()
    whole[own, :] = members

    eye = (
        lax.broadcasted_iota(jnp.int32, (ne, ne), 0) == lax.broadcasted_iota(jnp.int32, (ne, ne), 1)
    ).astype(jnp.float32).astype(jnp.bfloat16)
    noise = lax.dot_general(
        eye, noise_ref[...], (((1,), (1,)), ((), ())), preferred_element_type=jnp.float32
    )
    block_of = cells // BLOCK
    region = jnp.full(cells.shape, region_ref[0], jnp.int32)
    for b in range(1, blocks):
        region = jnp.where(block_of == b, region_ref[b], region)
    masks = [region == m * nreg + i for i in range(nreg)]
    error = error_ref[...]
    observed = observed_ref[...]

    for copy in swaps:
        copy.wait()
    values = vals[...].astype(jnp.float32)
    predicted = values + 0.2 * values * values * values
    pmean = jnp.sum(predicted, axis=0, keepdims=True) / ne
    inverse = 1.0 / error
    sens = (predicted - pmean) * inverse
    innov = (observed - predicted) * inverse + noise
    square = jnp.sum(innov * innov, axis=0, keepdims=True)
    joined = jnp.concatenate([sens, innov], axis=0).astype(jnp.bfloat16)
    masked = jnp.concatenate([jnp.where(mask, sens, 0.0) for mask in masks], axis=0).astype(jnp.bfloat16)
    partial = lax.dot_general(
        masked, joined, (((1,), (1,)), ((), ())), preferred_element_type=jnp.float32
    )
    diagonal = (
        lax.broadcasted_iota(jnp.int32, (ne, 2 * ne), 0)
        == lax.broadcasted_iota(jnp.int32, (ne, 2 * ne), 1)
    )
    partial = partial + jnp.concatenate(
        [
            jnp.where(
                diagonal,
                jnp.sum(jnp.where(mask, square, 0.0), axis=1, keepdims=True) / ne,
                0.0,
            )
            for mask in masks
        ],
        axis=0,
    )
    mine[...] = partial.astype(jnp.bfloat16)
    shares = []
    for offset in range(1, chips):
        shares.append(
            pltpu.make_async_remote_copy(
                src_ref=mine, dst_ref=slots.at[offset - 1],
                send_sem=g_send.at[offset - 1], recv_sem=g_recv.at[offset - 1],
                device_id=chip(offset), device_id_type=MESH,
            )
        )
        shares[-1].start()

    for copy in fetches:
        copy.wait()
    ensemble = whole[...].astype(jnp.float32)
    center = jnp.sum(ensemble, axis=0, keepdims=True) / ne
    anomaly = (ensemble - center).astype(jnp.bfloat16)

    total = mine[...].astype(jnp.float32)
    for offset, copy in enumerate(shares):
        copy.wait()
        total = total + slots[offset].astype(jnp.float32)

    damping = jnp.where(diagonal, ne - 1.0, 0.0)
    solved = []
    for i in range(nreg):
        system = total[i * ne : (i + 1) * ne] + damping
        rows = eliminate([system[g : g + 8] for g in range(0, ne, 8)], ne)
        solved.append(jnp.concatenate(rows, axis=0)[:, ne:])
    flipped = jnp.concatenate(solved, axis=0).T.astype(jnp.bfloat16)
    for to in range(nm):
        coeff[to] = flipped[to * half : (to + 1) * half]
    gives = []
    for offset in range(1, nm):
        gives.append(
            pltpu.make_async_remote_copy(
                src_ref=coeff.at[lax.rem(m + offset, nm)], dst_ref=coeff.at[nm + m],
                send_sem=c_send.at[offset - 1], recv_sem=c_recv.at[offset - 1],
                device_id=core(offset), device_id_type=MESH,
            )
        )
        gives[-1].start()
    kept = flipped[:half]
    for to in range(1, nm):
        kept = jnp.where(m == to, flipped[to * half : (to + 1) * half], kept)
    coeff[nm + m] = kept
    for copy in gives:
        copy.wait()
    regions = []
    for owner in range(nm):
        held = coeff[nm + owner]
        regions += [held[:, i * ne : (i + 1) * ne] for i in range(nreg)]
    for b in range(blocks):
        chosen = regions[0]
        for r in range(1, NLOC):
            chosen = jnp.where(region_ref[b] == r, regions[r], chosen)
        part = slice(b * BLOCK, (b + 1) * BLOCK)
        delta = jnp.dot(chosen, anomaly[:, part], preferred_element_type=jnp.float32)
        out_ref[:, part] = (members[:, part].astype(jnp.float32) + delta).astype(jnp.bfloat16)


def body(nz, nx, nm, members, observed, obs_error, obs_cells, perturbations, region_ids):
    half, width = members.shape
    count = observed.shape[0]
    ne = half * nm
    rows = NLOC // nm * ne
    chips = nz * nx
    vmem = pl.BlockSpec(memory_space=pltpu.VMEM)
    dma = pltpu.SemaphoreType.DMA
    return pl.pallas_call(
        functools.partial(kernel, nz, nx, nm),
        out_shape=jax.ShapeDtypeStruct(members.shape, members.dtype),
        in_specs=[pl.BlockSpec(memory_space=pltpu.SMEM)] + [vmem] * 5,
        out_specs=vmem,
        scratch_shapes=[
            pltpu.VMEM((ne, count), jnp.bfloat16),
            pltpu.VMEM((ne, width), jnp.bfloat16),
            pltpu.VMEM((rows, 2 * ne), jnp.bfloat16),
            pltpu.VMEM((chips - 1, rows, 2 * ne), jnp.bfloat16),
            pltpu.VMEM((2 * nm, half, rows), jnp.bfloat16),
            dma((nm - 1,)), dma((nm - 1,)), dma((nm - 1,)), dma((nm - 1,)),
            dma((chips - 1,)), dma((chips - 1,)), dma((nm - 1,)), dma((nm - 1,)),
        ],
        compiler_params=pltpu.CompilerParams(collective_id=0, has_side_effects=True),
    )(
        region_ids, members, observed.reshape(1, count), obs_error.reshape(1, count),
        obs_cells.reshape(1, count), perturbations,
    )


def solution(mesh):
    split = ("groups", "cells", "obs")
    in_specs = (P("mem", split), P(split), P(split), P(split), P(split, None), P(split))
    sizes = (mesh.shape["cells"], mesh.shape["obs"], mesh.shape["mem"])
    return jax.shard_map(
        functools.partial(body, *sizes), mesh=mesh, in_specs=in_specs, out_specs=P("mem", split), check_vma=False
    )
```

time: 130 us -> 22.8 us (0.18)
  waiting for transfers between devices: 53.3 us -> 0 us
  blocking collectives: 28.8 us -> 0 us
  other arithmetic: 24 us -> 0 us
  Pallas kernels: 0 us -> 19.3 us
  between operations: 14.3 us -> 0.01 us
  local copies, waits for them, and re-layouts: 6.69 us -> 3.3 us
  matrix products: 2.2 us -> 0 us
    psum x1 -> x0, waiting for transfers between devices: 53.3 us -> none  [body(): gram, misfit = lax.psum((gram, misfit), ('cells', 'mem'))]
    another operation x7 -> x0, other arithmetic: 21.8 us -> none  [the longest x4 11.9 us: solve_regions(): factor = jnp.linalg.cholesky(system)]
    pallas_call x0 -> x1, Pallas kernels: none -> 19.3 us  [body(): pl.pallas_call(functools.partial(kernel, nz, nx, nm), out_shape=jax.Shape...]
    psum x1 -> x0, blocking collectives: 16.3 us -> none  [body(): gram, misfit = lax.psum((gram, misfit), ('cells', 'mem'))]
    all_gather x2 -> x0, blocking collectives: 6.74 us -> none  [the longest x1 4.41 us: body(): mine = lax.all_gather(mine, 'obs', axis=0, tiled=True)]
    unnamed x1 -> x0, blocking collectives: 5.74 us -> none
    dot_general x5 -> x0, matrix products: 1.75 us -> none  [the longest x1 0.97 us: body(): lax.dot_general(masked, joined, (((0,), (0,)), ((), ())), preferred_eleme...]
    gather x2 -> x0, local copies, waits for them, and re-layouts: 1.44 us -> none  [body(): values = jnp.take(whole, my_cells, axis=1).T.astype(jnp.float32)]
  transfers between devices with their start and end apart: 2 -> 0, of which waited for: 1 -> 0; matrix products, arithmetic and copies ran while one was open for 1% -> 0% of each run, Pallas kernels for 0% -> 0%
where the time goes in v1:
time: 22.8 us; the launch traced here: 22.6 us
  Pallas kernels  19.3 us (85%)
  local copies, waits for them, and re-layouts  3.3 us (14%)
    pallas_call x1, Pallas kernels, body(): pl.pallas_call(functools.partial(kernel, nz, nx, nm), out_shape=jax.Shape...  19.3 us
    unnamed x2, local copies, waits for them, and re-layouts  3.3 us

profile of v1, /device:TPU:0, one launch (start us, length us, event | category | flops | bytes accessed | tf_op | source)
XLA Modules:
  0.0 22.6 jit_solution(1804638637750162079)
XLA Ops:
  0.0 1.7 %copy.7.noise_ref = bf16[1024,64]{1,0:T(8,128)(2,1)} copy(bf16[1024,64]{0,1:T(8,128)(2,1)} %param.10) | data formatting | bytes 262144 | tf_op args[4]
  1.7 19.3 %shard_map.64 = bf16[32,2048]{1,0:T(8,128)(2,1)} custom-call(s32[4]{0:T(128)} %region_ref.1, bf16[32,2048]{1,0:T(8,128)(2,1)} %members_ref.1, f32[1,1024]{1,0:T(1,128)} %bitcast.3, f32[1,1024]{1,0:T(1,128)} %bitcast.4, s32[1,1024]{1,0:T(1,128)} %bitcast.5, bf16[1024,64]{1,0:T(8,128)(2,1)} %copy.7.noise_ref), custom_call_target="tpu_custom_call" | custom-call | tf_op jit(solution)/shard_map/pallas_call | solution.py:221
  21.1 1.6 %copy.9 = bf16[32,2048]{1,0:T(8,128)(2,1)} copy(bf16[32,2048]{1,0:T(8,128)(2,1)} %shard_map.64) | data formatting | bytes 262144

commit v2 on v1

v2 whole, which is shorter than its diff:
```python
import functools

import jax
import jax.numpy as jnp
from jax import lax
from jax.experimental import pallas as pl
from jax.experimental.pallas import tpu as pltpu
from jax.sharding import PartitionSpec as P

BLOCK = 512
NLOC = 4
LANE = 128
NE_GROUPS = 4
MESH = pl.DeviceIdType.MESH


def gather_lanes(table, cells):
    rows, width = table.shape
    columns = []
    for start in range(0, cells.shape[1], LANE):
        index = cells[:, start : start + LANE]
        low = jnp.broadcast_to(index % LANE, (rows, LANE))
        high = jnp.broadcast_to(index // LANE, (rows, LANE))
        total = None
        for part in range(width // LANE):
            found = jnp.take_along_axis(
                table[:, part * LANE : (part + 1) * LANE], low, axis=1, mode="promise_in_bounds"
            )
            total = found if total is None else jnp.where(high == part, found, total)
        columns.append(total)
    return jnp.concatenate(columns, axis=1)


def eliminate(rows, ne):
    groups = len(rows)
    sub = lax.broadcasted_iota(jnp.int32, rows[0].shape, 0)
    for block in range(groups):
        base = block * 8
        cols = [
            [jnp.broadcast_to(rows[g][:, base + j : base + j + 1], rows[g].shape) for g in range(groups)]
            for j in range(8)
        ]
        for j in range(8):
            inv = 1.0 / cols[j][block][j : j + 1, :]
            here = sub == j
            for l in range(j + 1, 8):
                factor = cols[l][block][j : j + 1, :] * inv
                for g in range(groups):
                    new = cols[l][g] - cols[j][g] * factor
                    cols[l][g] = jnp.where(here, factor, new) if g == block else new
            pivot_row = rows[block][j : j + 1, :] * inv
            for g in range(groups):
                new = rows[g] - cols[j][g] * pivot_row
                rows[g] = jnp.where(here, pivot_row, new) if g == block else new
    return rows


def kernel(
    nz, nx, nm, region_ref, members_ref, observed_ref, error_ref, cells_ref, noise_ref, out_ref,
    vals, whole, mine, slots, give, coeff,
    v_send, v_recv, w_send, w_recv, g_send, g_recv, c_send, c_recv,
):
    z, x, m = lax.axis_index("cells"), lax.axis_index("obs"), lax.axis_index("mem")
    half = members_ref.shape[0]
    ne = half * nm
    nreg = NLOC // nm
    chips = nz * nx
    blocks = region_ref.shape[0]

    groups = NE_GROUPS
    cols = ne // groups
    slices = nreg * groups
    here = z * nx + x
    slice_id = lax.rem(here, slices)

    def device(index, core):
        return {"cells": index // nx, "obs": lax.rem(index, nx), "mem": core}

    def chip(offset):
        return lax.rem(here + offset, chips)

    def core(offset):
        return lax.rem(m + offset, nm)

    barrier = pltpu.get_barrier_semaphore()
    for offset in range(chips):
        for step in range(nm):
            if offset or step:
                pl.semaphore_signal(
                    barrier, inc=1, device_id=device(chip(offset), core(step)), device_id_type=MESH
                )

    own = pl.ds(pl.multiple_of(m * half, half), half)
    cells = cells_ref[...]
    members = members_ref[...]
    vals[own, :] = gather_lanes(members.astype(jnp.float32), cells).astype(jnp.bfloat16)
    whole[own, :] = members
    block_of = cells // BLOCK
    region = jnp.full(cells.shape, region_ref[0], jnp.int32)
    for b in range(1, blocks):
        region = jnp.where(block_of == b, region_ref[b], region)
    weights = [jnp.where(region == m * nreg + i, 1.0, 0.0) for i in range(nreg)]
    inverse = 1.0 / error_ref[...]
    observed = observed_ref[...]

    pl.semaphore_wait(barrier, chips * nm - 1)
    swaps = []
    for offset in range(1, nm):
        swaps.append(
            pltpu.make_async_remote_copy(
                src_ref=vals.at[own], dst_ref=vals.at[own],
                send_sem=v_send.at[offset - 1], recv_sem=v_recv.at[offset - 1],
                device_id=device(here, core(offset)), device_id_type=MESH,
            )
        )
        swaps[-1].start()
    fetches = []
    for offset in range(1, nm):
        fetches.append(
            pltpu.make_async_remote_copy(
                src_ref=members_ref, dst_ref=whole.at[own],
                send_sem=w_send.at[offset - 1], recv_sem=w_recv.at[offset - 1],
                device_id=device(here, core(offset)), device_id_type=MESH,
            )
        )
        fetches[-1].start()
    noise = noise_ref[...].astype(jnp.float32)
    for copy in swaps:
        copy.wait()
    values = vals[...].astype(jnp.float32)
    predicted = values + 0.2 * values * values * values
    pmean = jnp.sum(predicted, axis=0, keepdims=True) / ne
    sens = (predicted - pmean) * inverse
    innov = (observed - predicted) * inverse + noise
    square = jnp.sum(innov * innov, axis=0, keepdims=True)
    joined = jnp.concatenate([sens, innov], axis=0).astype(jnp.bfloat16)
    masked = jnp.concatenate([sens * weight for weight in weights], axis=0).astype(jnp.bfloat16)
    partial = lax.dot_general(
        masked, joined, (((1,), (1,)), ((), ())), preferred_element_type=jnp.float32
    )
    diagonal = (
        lax.broadcasted_iota(jnp.int32, (ne, 2 * ne), 0)
        == lax.broadcasted_iota(jnp.int32, (ne, 2 * ne), 1)
    )
    partial = partial + jnp.concatenate(
        [
            jnp.where(
                diagonal,
                jnp.sum(square * weight, axis=1, keepdims=True) / ne,
                0.0,
            )
            for weight in weights
        ],
        axis=0,
    )
    fold = ne // 2
    for i in range(nreg):
        block = partial[i * ne : (i + 1) * ne]
        top, bottom = block[:fold], block[fold:]
        for k in range(groups):
            at = ne + k * cols
            mine[k * nreg + i] = jnp.concatenate(
                [top[:, :ne], bottom[:, fold:ne], top[:, at : at + cols], bottom[:, at : at + cols]], axis=1
            ).astype(jnp.bfloat16)
    shares = []
    for offset in range(1, chips):
        shares.append(
            pltpu.make_async_remote_copy(
                src_ref=mine.at[lax.rem(chip(offset), slices)], dst_ref=slots.at[offset - 1],
                send_sem=g_send.at[offset - 1], recv_sem=g_recv.at[offset - 1],
                device_id=device(chip(offset), m), device_id_type=MESH,
            )
        )
        shares[-1].start()

    for copy in fetches:
        copy.wait()
    ensemble = whole[...].astype(jnp.float32)
    center = jnp.sum(ensemble, axis=0, keepdims=True) / ne
    anomaly = (ensemble - center).astype(jnp.bfloat16)

    total = mine[slice_id].astype(jnp.float32)
    for offset, copy in enumerate(shares):
        copy.wait()
        total = total + slots[offset].astype(jnp.float32)

    pad = jnp.zeros((fold, ne - cols), jnp.float32)
    corner = total[:, fold:ne]
    system = jnp.concatenate(
        [
            jnp.concatenate([total[:, :ne], total[:, 3 * fold : 3 * fold + cols], pad], axis=1),
            jnp.concatenate([corner.T, total[:, ne : 3 * fold], total[:, 3 * fold + cols :], pad], axis=1),
        ],
        axis=0,
    )
    system = system + jnp.where(diagonal, ne - 1.0, 0.0)
    rows = eliminate([system[g : g + 8] for g in range(0, ne, 8)], ne)
    flipped = jnp.concatenate(rows, axis=0).T[ne : ne + cols]
    give[...] = jnp.concatenate([flipped, jnp.zeros_like(flipped)], axis=1).astype(jnp.bfloat16)

    per_core = groups // nm
    group = slice_id // nreg
    taker = group // per_core
    place = coeff.at[
        m * nreg + lax.rem(slice_id, nreg), pl.ds(pl.multiple_of(lax.rem(group, per_core) * cols, cols), cols)
    ]
    source = m * (nreg * per_core) + lax.rem(slice_id, nreg * per_core)
    first = here - slice_id
    remote = [
        pltpu.make_async_remote_copy(
            src_ref=give, dst_ref=place, send_sem=c_send.at[offset], recv_sem=c_recv.at[source],
            device_id=device(first + lax.rem(slice_id + offset, slices), taker), device_id_type=MESH,
        )
        for offset in range(slices)
    ]
    for copy in remote[1:]:
        copy.start()

    @pl.when(taker == m)
    def _():
        pltpu.make_async_copy(give, place, c_recv.at[source]).start()

    @pl.when(taker != m)
    def _():
        remote[0].start()
        remote[0].wait_send()

    for copy in remote[1:]:
        copy.wait_send()
    for owner in range(NLOC * per_core):
        pltpu.make_async_copy(give, coeff.at[owner // per_core, pl.ds(0, cols)], c_recv.at[owner]).wait()
    regions = [coeff[r][:, :ne] for r in range(NLOC)]
    for b in range(blocks):
        chosen = regions[0]
        for r in range(1, NLOC):
            chosen = jnp.where(region_ref[b] == r, regions[r], chosen)
        part = slice(b * BLOCK, (b + 1) * BLOCK)
        delta = jnp.dot(chosen, anomaly[:, part], preferred_element_type=jnp.float32)
        out_ref[:, part] = (members[:, part].astype(jnp.float32) + delta).astype(jnp.bfloat16)


def body(nz, nx, nm, members, observed, obs_error, obs_cells, perturbations, region_ids):
    half, width = members.shape
    count = observed.shape[0]
    ne = half * nm
    slices = NLOC // nm * NE_GROUPS
    chips = nz * nx
    vmem = pl.BlockSpec(memory_space=pltpu.VMEM)
    dma = pltpu.SemaphoreType.DMA
    return pl.pallas_call(
        functools.partial(kernel, nz, nx, nm),
        out_shape=jax.ShapeDtypeStruct(members.shape, members.dtype),
        in_specs=[pl.BlockSpec(memory_space=pltpu.SMEM)] + [vmem] * 5,
        out_specs=vmem,
        scratch_shapes=[
            pltpu.VMEM((ne, count), jnp.bfloat16),
            pltpu.VMEM((ne, width), jnp.bfloat16),
            pltpu.VMEM((slices, ne // 2, 2 * ne), jnp.bfloat16),
            pltpu.VMEM((chips - 1, ne // 2, 2 * ne), jnp.bfloat16),
            pltpu.VMEM((ne // NE_GROUPS, 2 * ne), jnp.bfloat16),
            pltpu.VMEM((NLOC, half, 2 * ne), jnp.bfloat16),
            dma((nm - 1,)), dma((nm - 1,)), dma((nm - 1,)), dma((nm - 1,)),
            dma((chips - 1,)), dma((chips - 1,)), dma((slices,)), dma((NLOC * NE_GROUPS // nm,)),
        ],
        compiler_params=pltpu.CompilerParams(collective_id=0, has_side_effects=True),
    )(
        region_ids, members, observed.reshape(1, count), obs_error.reshape(1, count),
        obs_cells.reshape(1, count), perturbations.T,
    )


def solution(mesh):
    split = ("groups", "cells", "obs")
    in_specs = (P("mem", split), P(split), P(split), P(split), P(split, None), P(split))
    sizes = (mesh.shape["cells"], mesh.shape["obs"], mesh.shape["mem"])
    return jax.shard_map(
        functools.partial(body, *sizes), mesh=mesh, in_specs=in_specs, out_specs=P("mem", split), check_vma=False
    )
```

time: 22.8 us -> 20.8 us (0.912)
  the two profiles are of different devices: /device:TPU:0 before, /device:TPU:1 now
where the time goes in v2:
time: 20.8 us; the launch traced here: 20.6 us
  Pallas kernels  19.1 us (92%)
  local copies, waits for them, and re-layouts  1.57 us (8%)
    pallas_call x1, Pallas kernels, body(): pl.pallas_call(functools.partial(kernel, nz, nx, nm), out_shape=jax.Shape...  19.1 us
    unnamed x1, local copies, waits for them, and re-layouts  1.57 us

profile of v2, /device:TPU:1, one launch (start us, length us, event | category | flops | bytes accessed | tf_op | source)
XLA Modules:
  0.0 20.6 jit_solution(1160234568686283546)
XLA Ops:
  0.0 19.1 %shard_map.64 = bf16[32,2048]{1,0:T(8,128)(2,1)} custom-call(s32[4]{0:T(128)} %region_ref.1, bf16[32,2048]{1,0:T(8,128)(2,1)} %members_ref.1, f32[1,1024]{1,0:T(1,128)} %bitcast.5, f32[1,1024]{1,0:T(1,128)} %bitcast.6, s32[1,1024]{1,0:T(1,128)} %bitcast.7, bf16[64,1024]{1,0:T(8,128)(2,1)} %bitcast.4), custom_call_target="tpu_custom_call" | custom-call | tf_op jit(solution)/shard_map/pallas_call | solution.py:250
  19.1 1.6 %copy.8 = bf16[32,2048]{1,0:T(8,128)(2,1)} copy(bf16[32,2048]{1,0:T(8,128)(2,1)} %shard_map.64) | data formatting | bytes 262144

commit v3 on v2

--- a/solution.py
+++ b/solution.py
@@ -56,16 +56,17 @@
 
 
 def kernel(
-    nz, nx, nm, region_ref, members_ref, observed_ref, error_ref, cells_ref, noise_ref, out_ref,
+    nz, nx, nm, region_any, members_any, observed_any, error_any, cells_any, noise_any, out_ref,
+    region_ref, observed_ref, error_ref, cells_ref, noise_ref, loads,
     vals, whole, mine, slots, give, coeff,
     v_send, v_recv, w_send, w_recv, g_send, g_recv, c_send, c_recv,
 ):
     z, x, m = lax.axis_index("cells"), lax.axis_index("obs"), lax.axis_index("mem")
-    half = members_ref.shape[0]
+    half = members_any.shape[0]
     ne = half * nm
     nreg = NLOC // nm
     chips = nz * nx
-    blocks = region_ref.shape[0]
+    blocks = region_any.shape[0]
 
     groups = NE_GROUPS
     cols = ne // groups
@@ -91,10 +92,24 @@
                 )
 
     own = pl.ds(pl.multiple_of(m * half, half), half)
+    staged = [
+        pltpu.make_async_copy(source, target, loads.at[i])
+        for i, (source, target) in enumerate(
+            [
+                (cells_any, cells_ref), (members_any, whole.at[own]), (region_any, region_ref),
+                (error_any, error_ref), (observed_any, observed_ref), (noise_any, noise_ref),
+            ]
+        )
+    ]
+    for copy in staged:
+        copy.start()
+    for copy in staged[:2]:
+        copy.wait()
     cells = cells_ref[...]
-    members = members_ref[...]
+    members = whole[own, :]
     vals[own, :] = gather_lanes(members.astype(jnp.float32), cells).astype(jnp.bfloat16)
-    whole[own, :] = members
+    for copy in staged[2:]:
+        copy.wait()
     block_of = cells // BLOCK
     region = jnp.full(cells.shape, region_ref[0], jnp.int32)
     for b in range(1, blocks):
@@ -118,7 +133,7 @@
     for offset in range(1, nm):
         fetches.append(
             pltpu.make_async_remote_copy(
-                src_ref=members_ref, dst_ref=whole.at[own],
+                src_ref=whole.at[own], dst_ref=whole.at[own],
                 send_sem=w_send.at[offset - 1], recv_sem=w_recv.at[offset - 1],
                 device_id=device(here, core(offset)), device_id_type=MESH,
             )
@@ -249,10 +264,16 @@
     dma = pltpu.SemaphoreType.DMA
     return pl.pallas_call(
         functools.partial(kernel, nz, nx, nm),
-        out_shape=jax.ShapeDtypeStruct(members.shape, members.dtype),
-        in_specs=[pl.BlockSpec(memory_space=pltpu.SMEM)] + [vmem] * 5,
+        out_shape=pltpu.VMEM(members.shape, members.dtype),
+        in_specs=[pl.BlockSpec(memory_space=pl.ANY)] * 6,
         out_specs=vmem,
         scratch_shapes=[
+            pltpu.SMEM(region_ids.shape, jnp.int32),
+            pltpu.VMEM((1, count), jnp.float32),
+            pltpu.VMEM((1, count), jnp.float32),
+            pltpu.VMEM((1, count), jnp.int32),
+            pltpu.VMEM((ne, count), jnp.bfloat16),
+            dma((6,)),
             pltpu.VMEM((ne, count), jnp.bfloat16),
             pltpu.VMEM((ne, width), jnp.bfloat16),
             pltpu.VMEM((slices, ne // 2, 2 * ne), jnp.bfloat16),

time: 20.8 us -> 18.3 us (0.88)
  Pallas kernels: 19.1 us -> 17.4 us
  local copies, waits for them, and re-layouts: 1.57 us -> 0.66 us
    pallas_call x1, Pallas kernels: 19.1 us -> 17.4 us  [body(): pl.pallas_call(functools.partial(kernel, nz, nx, nm), out_shape=pltpu.VME...]
    unnamed x1, local copies, waits for them, and re-layouts: 1.57 us -> 0.66 us
where the time goes in v3:
time: 18.3 us; the launch traced here: 18.1 us
  Pallas kernels  17.4 us (95%)
  local copies, waits for them, and re-layouts  0.66 us (4%)
    pallas_call x1, Pallas kernels, body(): pl.pallas_call(functools.partial(kernel, nz, nx, nm), out_shape=pltpu.VME...  17.4 us
    unnamed x1, local copies, waits for them, and re-layouts  0.66 us

profile of v3, /device:TPU:1, one launch (start us, length us, event | category | flops | bytes accessed | tf_op | source)
XLA Modules:
  0.0 18.1 jit_solution(14347079855141383676)
XLA Ops:
  0.0 17.4 %shard_map.64 = bf16[32,2048]{1,0:T(8,128)(2,1)S(1)} custom-call(s32[4]{0:T(128)} %region_any.1, bf16[32,2048]{1,0:T(8,128)(2,1)} %members_any.1, f32[1,1024]{1,0:T(1,128)} %bitcast.5, f32[1,1024]{1,0:T(1,128)} %bitcast.6, s32[1,1024]{1,0:T(1,128)} %bitcast.7, bf16[64,1024]{1,0:T(8,128)(2,1)} %bitcast.4), custom_call_target="tpu_custom_call" | custom-call | tf_op jit(solution)/shard_map/pallas_call | solution.py:265
  17.4 0.7 %copy.8 = bf16[32,2048]{1,0:T(8,128)(2,1)} copy(bf16[32,2048]{1,0:T(8,128)(2,1)S(1)} %shard_map.64) | data formatting | bytes 262144

commit v4 on v3

--- a/solution.py
+++ b/solution.py
@@ -10,7 +10,6 @@
 BLOCK = 512
 NLOC = 4
 LANE = 128
-NE_GROUPS = 4
 MESH = pl.DeviceIdType.MESH
 
 
@@ -68,9 +67,7 @@
     chips = nz * nx
     blocks = region_any.shape[0]
 
-    groups = NE_GROUPS
-    cols = ne // groups
-    slices = nreg * groups
+    slices = nreg
     here = z * nx + x
     slice_id = lax.rem(here, slices)
 
@@ -168,15 +165,8 @@
         ],
         axis=0,
     )
-    fold = ne // 2
     for i in range(nreg):
-        block = partial[i * ne : (i + 1) * ne]
-        top, bottom = block[:fold], block[fold:]
-        for k in range(groups):
-            at = ne + k * cols
-            mine[k * nreg + i] = jnp.concatenate(
-                [top[:, :ne], bottom[:, fold:ne], top[:, at : at + cols], bottom[:, at : at + cols]], axis=1
-            ).astype(jnp.bfloat16)
+        mine[i] = partial[i * ne : (i + 1) * ne].astype(jnp.bfloat16)
     shares = []
     for offset in range(1, chips):
         shares.append(
@@ -199,51 +189,31 @@
         copy.wait()
         total = total + slots[offset].astype(jnp.float32)
 
-    pad = jnp.zeros((fold, ne - cols), jnp.float32)
-    corner = total[:, fold:ne]
-    system = jnp.concatenate(
-        [
-            jnp.concatenate([total[:, :ne], total[:, 3 * fold : 3 * fold + cols], pad], axis=1),
-            jnp.concatenate([corner.T, total[:, ne : 3 * fold], total[:, 3 * fold + cols :], pad], axis=1),
-        ],
-        axis=0,
-    )
-    system = system + jnp.where(diagonal, ne - 1.0, 0.0)
+    system = total + jnp.where(diagonal, ne - 1.0, 0.0)
     rows = eliminate([system[g : g + 8] for g in range(0, ne, 8)], ne)
-    flipped = jnp.concatenate(rows, axis=0).T[ne : ne + cols]
+    flipped = jnp.concatenate(rows, axis=0).T[ne:]
     give[...] = jnp.concatenate([flipped, jnp.zeros_like(flipped)], axis=1).astype(jnp.bfloat16)
 
-    per_core = groups // nm
-    group = slice_id // nreg
-    taker = group // per_core
-    place = coeff.at[
-        m * nreg + lax.rem(slice_id, nreg), pl.ds(pl.multiple_of(lax.rem(group, per_core) * cols, cols), cols)
-    ]
-    source = m * (nreg * per_core) + lax.rem(slice_id, nreg * per_core)
-    first = here - slice_id
-    remote = [
-        pltpu.make_async_remote_copy(
-            src_ref=give, dst_ref=place, send_sem=c_send.at[offset], recv_sem=c_recv.at[source],
-            device_id=device(first + lax.rem(slice_id + offset, slices), taker), device_id_type=MESH,
-        )
-        for offset in range(slices)
-    ]
-    for copy in remote[1:]:
-        copy.start()
-
-    @pl.when(taker == m)
-    def _():
-        pltpu.make_async_copy(give, place, c_recv.at[source]).start()
-
-    @pl.when(taker != m)
-    def _():
-        remote[0].start()
-        remote[0].wait_send()
-
-    for copy in remote[1:]:
+    owned = m * nreg + slice_id
+    gifts = []
+    for offset in range(slices):
+        for step in range(nm):
+            if offset or step:
+                gifts.append(
+                    pltpu.make_async_remote_copy(
+                        src_ref=give.at[pl.ds(pl.multiple_of(core(step) * half, half), half)],
+                        dst_ref=coeff.at[owned],
+                        send_sem=c_send.at[offset * nm + step], recv_sem=c_recv.at[owned],
+                        device_id=device(here - slice_id + lax.rem(slice_id + offset, slices), core(step)),
+                        device_id_type=MESH,
+                    )
+                )
+                gifts[-1].start()
+    pltpu.make_async_copy(give.at[own], coeff.at[owned], c_recv.at[owned]).start()
+    for copy in gifts:
         copy.wait_send()
-    for owner in range(NLOC * per_core):
-        pltpu.make_async_copy(give, coeff.at[owner // per_core, pl.ds(0, cols)], c_recv.at[owner]).wait()
+    for r in range(NLOC):
+        pltpu.make_async_copy(give.at[pl.ds(0, half)], coeff.at[r], c_recv.at[r]).wait()
     regions = [coeff[r][:, :ne] for r in range(NLOC)]
     for b in range(blocks):
         chosen = regions[0]
@@ -258,7 +228,7 @@
     half, width = members.shape
     count = observed.shape[0]
     ne = half * nm
-    slices = NLOC // nm * NE_GROUPS
+    slices = NLOC // nm
     chips = nz * nx
     vmem = pl.BlockSpec(memory_space=pltpu.VMEM)
     dma = pltpu.SemaphoreType.DMA
@@ -276,12 +246,12 @@
             dma((6,)),
             pltpu.VMEM((ne, count), jnp.bfloat16),
             pltpu.VMEM((ne, width), jnp.bfloat16),
-            pltpu.VMEM((slices, ne // 2, 2 * ne), jnp.bfloat16),
-            pltpu.VMEM((chips - 1, ne // 2, 2 * ne), jnp.bfloat16),
-            pltpu.VMEM((ne // NE_GROUPS, 2 * ne), jnp.bfloat16),
+            pltpu.VMEM((slices, ne, 2 * ne), jnp.bfloat16),
+            pltpu.VMEM((chips - 1, ne, 2 * ne), jnp.bfloat16),
+            pltpu.VMEM((ne, 2 * ne), jnp.bfloat16),
             pltpu.VMEM((NLOC, half, 2 * ne), jnp.bfloat16),
             dma((nm - 1,)), dma((nm - 1,)), dma((nm - 1,)), dma((nm - 1,)),
-            dma((chips - 1,)), dma((chips - 1,)), dma((slices,)), dma((NLOC * NE_GROUPS // nm,)),
+            dma((chips - 1,)), dma((chips - 1,)), dma((slices * nm,)), dma((NLOC,)),
         ],
         compiler_params=pltpu.CompilerParams(collective_id=0, has_side_effects=True),
     )(

time: 18.3 us -> 17.2 us (0.940)
  the two profiles are of different devices: /device:TPU:1 before, /device:TPU:0 now
where the time goes in v4:
time: 17.2 us; the launch traced here: 17.1 us
  Pallas kernels  16.4 us (95%)
  local copies, waits for them, and re-layouts  0.66 us (4%)
    pallas_call x1, Pallas kernels, body(): pl.pallas_call(functools.partial(kernel, nz, nx, nm), out_shape=pltpu.VME...  16.4 us
    unnamed x1, local copies, waits for them, and re-layouts  0.66 us

profile of v4, /device:TPU:0, one launch (start us, length us, event | category | flops | bytes accessed | tf_op | source)
XLA Modules:
  0.0 17.1 jit_solution(5085044663713758246)
XLA Ops:
  0.0 16.4 %shard_map.64 = bf16[32,2048]{1,0:T(8,128)(2,1)S(1)} custom-call(s32[4]{0:T(128)} %region_any.1, bf16[32,2048]{1,0:T(8,128)(2,1)} %members_any.1, f32[1,1024]{1,0:T(1,128)} %bitcast.5, f32[1,1024]{1,0:T(1,128)} %bitcast.6, s32[1,1024]{1,0:T(1,128)} %bitcast.7, bf16[64,1024]{1,0:T(8,128)(2,1)} %bitcast.4), custom_call_target="tpu_custom_call" | custom-call | tf_op jit(solution)/shard_map/pallas_call | solution.py:235
  16.4 0.7 %copy.8 = bf16[32,2048]{1,0:T(8,128)(2,1)} copy(bf16[32,2048]{1,0:T(8,128)(2,1)S(1)} %shard_map.64) | data formatting | bytes 262144

commit v5 on v4

--- a/solution.py
+++ b/solution.py
@@ -33,21 +33,23 @@
 def eliminate(rows, ne):
     groups = len(rows)
     sub = lax.broadcasted_iota(jnp.int32, rows[0].shape, 0)
-    for block in range(groups):
-        base = block * 8
+    width = 4
+    for base in range(0, ne, width):
+        block, first = base // 8, base % 8
         cols = [
             [jnp.broadcast_to(rows[g][:, base + j : base + j + 1], rows[g].shape) for g in range(groups)]
-            for j in range(8)
+            for j in range(width)
         ]
-        for j in range(8):
-            inv = 1.0 / cols[j][block][j : j + 1, :]
-            here = sub == j
-            for l in range(j + 1, 8):
-                factor = cols[l][block][j : j + 1, :] * inv
+        for j in range(width):
+            at = first + j
+            inv = 1.0 / cols[j][block][at : at + 1, :]
+            here = sub == at
+            for l in range(j + 1, width):
+                factor = cols[l][block][at : at + 1, :] * inv
                 for g in range(groups):
                     new = cols[l][g] - cols[j][g] * factor
                     cols[l][g] = jnp.where(here, factor, new) if g == block else new
-            pivot_row = rows[block][j : j + 1, :] * inv
+            pivot_row = rows[block][at : at + 1, :] * inv
             for g in range(groups):
                 new = rows[g] - cols[j][g] * pivot_row
                 rows[g] = jnp.where(here, pivot_row, new) if g == block else new

time: 17.2 us -> 18.2 us (1.058)
  Pallas kernels: 16.4 us -> 17.3 us
    pallas_call x1, Pallas kernels: 16.4 us -> 17.3 us  [body(): pl.pallas_call(functools.partial(kernel, nz, nx, nm), out_shape=pltpu.VME...]
where the time goes in v5:
time: 18.2 us; the launch traced here: 18 us
  Pallas kernels  17.3 us (95%)
  local copies, waits for them, and re-layouts  0.66 us (4%)
    pallas_call x1, Pallas kernels, body(): pl.pallas_call(functools.partial(kernel, nz, nx, nm), out_shape=pltpu.VME...  17.3 us
    unnamed x1, local copies, waits for them, and re-layouts  0.66 us

profile of v5, /device:TPU:0, one launch (start us, length us, event | category | flops | bytes accessed | tf_op | source)
XLA Modules:
  0.0 18.0 jit_solution(13940247605445119835)
XLA Ops:
  0.0 17.3 %shard_map.64 = bf16[32,2048]{1,0:T(8,128)(2,1)S(1)} custom-call(s32[4]{0:T(128)} %region_any.1, bf16[32,2048]{1,0:T(8,128)(2,1)} %members_any.1, f32[1,1024]{1,0:T(1,128)} %bitcast.5, f32[1,1024]{1,0:T(1,128)} %bitcast.6, s32[1,1024]{1,0:T(1,128)} %bitcast.7, bf16[64,1024]{1,0:T(8,128)(2,1)} %bitcast.4), custom_call_target="tpu_custom_call" | custom-call | tf_op jit(solution)/shard_map/pallas_call | solution.py:237
  17.3 0.7 %copy.8 = bf16[32,2048]{1,0:T(8,128)(2,1)} copy(bf16[32,2048]{1,0:T(8,128)(2,1)S(1)} %shard_map.64) | data formatting | bytes 262144
